TPU v7x, 32 devices: a whole 2x2x4 slice. The times are simulated.
32 devices in a mesh: seq: 8 (over y, x, core), tensor: 4 (over z).
Axes of the slice: x: 2, y: 2, z: 4, core: 2. Of those that a mesh axis runs over, the one named last changes fastest.
Arguments:
- tokens: bfloat16 [1024, 16384], P('seq', 'tensor'), may hold values from -100 to 100
- norm_gain: float32 [16384], P('tensor'), may hold values from 0.5 to 1.5
- projection_weight: bfloat16 [2048, 16384], P('tensor', 'seq'), may hold values from -1.5 to 1.5
- panel_index: int32 [1], replicated, may hold values from 0 to 31
Outputs:
- gram: float32 [16384, 16384], P('seq', 'tensor')
- factor_panel: bfloat16 [16384, 512], P('seq')
- projected: float32 [2048, 512], P('tensor', 'seq')
All inputs are finite; a program needn't handle non-finite values.
Results may differ from a plain program's by a relative error of at most 0.0057.
Values may be sent and summed in bfloat16 or wider, within the bound.
No kernel may reach another device: no remote copies, remote signals or barrier semaphores. Data moves between devices by JAX's collectives and lax.ppermute only.
A program may use at most 128 MiB of HBM per device.

v0:
```python
import jax
import jax.numpy as jnp
from jax import lax
from jax.sharding import PartitionSpec as P

D = 16384
PANEL = 512
epsilon = 1e-05
damping = 0.1


def broadcast(value, axis, source):
    kept = jnp.where(lax.axis_index(axis) == source, value, 0).astype(value.dtype)
    return lax.psum(kept, axis)


def on_device(tokens, norm_gain, projection_weight, panel_index):
    token_values = tokens.astype(jnp.float32)
    squares = lax.psum(jnp.sum(token_values * token_values, axis=1), "tensor")
    scaled = token_values * lax.rsqrt(squares / D + epsilon)[:, None] * norm_gain[None, :]
    normed = scaled.astype(jnp.bfloat16)
    column_width = normed.shape[1]
    row_width = column_width * lax.axis_size("tensor") // lax.axis_size("seq")
    blocks = column_width // row_width
    seq_index = lax.axis_index("seq")
    tensor_index = lax.axis_index("tensor")
    columns = lax.all_gather(normed, "seq", axis=0, tiled=True)
    local_rows = lax.dynamic_slice_in_dim(columns, seq_index % blocks * row_width, row_width, 1)
    row_part = broadcast(local_rows, "tensor", seq_index // blocks)
    tokens_all = columns.shape[0]
    gram_tile = (
        lax.dot_general(
            row_part, columns, (((0,), (0,)), ((), ())), preferred_element_type=jnp.float32
        )
        / tokens_all
    )
    normed_wide = normed.astype(jnp.float32)
    trace_sum = lax.psum(jnp.sum(normed_wide * normed_wide), ("seq", "tensor")) / tokens_all
    diag_shift = damping * trace_sum / D
    row_ids = seq_index * row_width + lax.iota(jnp.int32, row_width)
    col_ids = tensor_index * column_width + lax.iota(jnp.int32, column_width)
    shifted = gram_tile + jnp.where(
        row_ids[:, None] == col_ids[None, :], diag_shift, jnp.float32(0.0)
    )
    panel_start = panel_index[0] * PANEL
    owner_column = panel_start // column_width
    offset = panel_start - owner_column * column_width
    panel_rows = lax.dynamic_slice_in_dim(shifted, offset, PANEL, 1)
    panel_tokens = lax.dynamic_slice_in_dim(columns, offset, PANEL, 1)
    diag_block = (
        lax.dot_general(
            panel_tokens, panel_tokens, (((0,), (0,)), ((), ())), preferred_element_type=jnp.float32
        )
        / tokens_all
    )
    panel_ids = lax.iota(jnp.int32, PANEL)
    diag_block = diag_block + jnp.where(
        panel_ids[:, None] == panel_ids[None, :], diag_shift, jnp.float32(0.0)
    )
    identity = jnp.eye(PANEL, dtype=jnp.float32)
    diag_block = jnp.where(tensor_index == owner_column, diag_block, identity)
    factor = jnp.linalg.cholesky(diag_block)
    solved = lax.linalg.triangular_solve(
        factor, panel_rows, left_side=False, lower=True, transpose_a=True
    )
    whitened_rows = solved.astype(jnp.bfloat16)
    whitened_full = broadcast(whitened_rows, "tensor", owner_column)
    partial_value = jnp.dot(projection_weight, whitened_full, preferred_element_type=jnp.float32)
    projected = lax.psum_scatter(partial_value, "seq", scatter_dimension=1, tiled=True)
    return (shifted, whitened_full, projected)


def solution(mesh):
    placed = (P("seq", "tensor"), P("tensor"), P("tensor", "seq"), P())
    return jax.shard_map(
        on_device,
        mesh=mesh,
        in_specs=placed,
        out_specs=(P("seq", "tensor"), P("seq", None), P("tensor", "seq")),
        check_vma=False,
    )
```

profile of v0, /device:TPU:0, one launch (start us, length us, event | category | flops | bytes accessed | tf_op | source)
XLA Modules:
  0.0 426.1 jit_solution(7215072890339092447)
XLA Ops:
  8.9 13.5 %psum.28 = f32[128]{0:T(128)S(1)} all-reduce(f32[128]{0:T(128)S(1)} %fusion.9), channel_id=1, replica_groups=mesh['seq'=8,'tensor'=4] {'tensor'}, use_global_device_ids=true, to_apply=%region_1.0 | all-reduce | flops 128 | bytes 1024 | tf_op jit(solution)/shard_map/psum | solution.py:19
  22.4 3.2 multiply_reduce_fusion
  25.7 39.0 %psum.30 = f32[]{:T(128)} all-reduce(f32[]{:T(128)} %get-tuple-element.26), channel_id=1, replica_groups=mesh['seq'=8,'tensor'=4] {'seq','tensor'}, use_global_device_ids=true, to_apply=%region_4.5 | all-reduce | flops 1 | bytes 8 | tf_op jit(solution)/shard_map/psum | solution.py:38
  67.2 11.8 %all-gather.2.cloned.1.call-done = bf16[1024,4096]{1,0:T(8,128)(2,1)} async-done(((bf16[128,4096]{1,0:T(8,128)(2,1)}), bf16[1024,4096]{1,0:T(8,128)(2,1)}) %all-gather.2.cloned.1.call-update) | async-done | bytes 8388624 | tf_op jit(solution)/shard_map/all_gather | solution.py:27
  79.0 5.5 %dynamic-slice_select_fusion = bf16[1024,2048]{1,0:T(8,128)(2,1)} fusion(bf16[1024,4096]{1,0:T(8,128)(2,1)} %all-gather.2.cloned.1.call-done, s32[]{:T(128)S(6)} %select_n.66, pred[]{:T(512)S(6)} %eq.56), kind=kLoop, calls=%fused_computation.3 | loop fusion | flops 2097152 | bytes 8388613 | tf_op jit(solution)/shard_map/jit(_where)/select_n | solution.py:13
  85.2 3.7 convert_select_fusion
  93.0 11.7 %cholesky.103 = f32[128,128]{1,0:T(8,128)S(1)} custom-call(f32[128,128]{1,0:T(8,128)S(1)} %cholesky.263), custom_call_target="Cholesky" | custom-call | tf_op jit(solution)/shard_map/jit(cholesky)/cholesky | solution.py:62
  105.3 9.8 %custom-call.30 = f32[1,128,128]{1,2,0:T(8,128)S(1)} custom-call(f32[1,128,128]{2,1,0:T(8,128)S(1)} %get-tuple-element.35), custom_call_target="InvertDiagBlocksLowerTriangular" | custom-call | tf_op jit(solution)/shard_map/jit(cholesky)/cholesky | solution.py:62
  118.5 11.7 %cholesky.215 = f32[128,128]{1,0:T(8,128)S(1)} custom-call(f32[128,128]{1,0:T(8,128)S(1)} %cholesky.267), custom_call_target="Cholesky" | custom-call | tf_op jit(solution)/shard_map/jit(cholesky)/cholesky | solution.py:62
  131.5 10.6 %custom-call.31 = f32[1,128,128]{1,2,0:T(8,128)} custom-call(f32[1,128,128]{2,1,0:T(8,128)S(1)} %get-tuple-element.33), custom_call_target="InvertDiagBlocksLowerTriangular" | custom-call | tf_op jit(solution)/shard_map/jit(cholesky)/cholesky | solution.py:62
  146.6 11.7 %cholesky.236 = f32[128,128]{1,0:T(8,128)S(1)} custom-call(f32[128,128]{1,0:T(8,128)S(1)} %cholesky.272), custom_call_target="Cholesky" | custom-call | tf_op jit(solution)/shard_map/jit(cholesky)/cholesky | solution.py:62
  158.4 9.8 %custom-call.32 = f32[1,128,128]{1,2,0:T(8,128)S(1)} custom-call(f32[1,128,128]{2,1,0:T(8,128)S(1)} %get-tuple-element.31), custom_call_target="InvertDiagBlocksLowerTriangular" | custom-call | tf_op jit(solution)/shard_map/jit(cholesky)/cholesky | solution.py:62
  169.9 11.9 %cholesky.253 = f32[128,128]{1,0:T(8,128)S(1)} custom-call(f32[128,128]{1,0:T(8,128)S(1)} %convolution_subtract_fusion.4), custom_call_target="Cholesky" | custom-call | tf_op jit(solution)/shard_map/jit(cholesky)/cholesky | solution.py:62
  188.9 14.3 %while.1 = (s32[]{:T(128)}, f32[512,512]{0,1:T(8,128)}, s32[4,2]{0,1:T(2,128)S(1)}, f32[4,128,128]{2,1,0:T(8,128)}, s32[]{:T(128)}) while((s32[]{:T(128)}, f32[512,512]{0,1:T(8,128)}, s32[4,2]{0,1:T(2,128)S(1)}, f32[4,128,128]{2,1,0:T(8,128)}, s32[]{:T(128)}) %tuple.34), condition=%wide.while_cond, body=%wide.while_body.sunk | while | flops 2 | bytes 393329 | solution.py:63
  203.2 40.1 %custom-call.33 = f32[4,128,128]{1,2,0:T(8,128)S(1)} custom-call(f32[4,128,128]{2,1,0:T(8,128)} %get-tuple-element.10), custom_call_target="InvertDiagBlocksLowerTriangular" | custom-call | tf_op jit(solution)/shard_map/triangular_solve | solution.py:63
  243.3 28.2 %select_add_fusion = f32[2048,4096]{1,0:T(8,128)} fusion(bf16[1024,2048]{1,0:T(8,128)(2,1)} %all-reduce.4.cloned.1.call-done, bf16[1024,4096]{1,0:T(8,128)(2,1)} %all-gather.2.cloned.1.call-done, f32[]{:T(128)S(6)} %div.54, s32[4096]{0:T(1024)S(1)} %iota_add_fusion, s32[2048]{0:T(1024)} %iota_add_fusion.1), kind=kOutput, calls=%fused_computation.2 | convolution fusion | flops 17213423616 | bytes 46161924 | tf_op jit(solution)/shard_map/dot_general | solution.py:32
  271.6 2.3 fusion.45
  273.9 3.1 convolution_subtract_fusion.1
  278.1 5.0 %convolution_subtract_fusion = f32[2048,128]{1,0:T(8,128)S(1)} fusion(f32[2048,128]{0,1:T(8,128)S(1)} %get-tuple-element.41, f32[2048,128]{0,1:T(8,128)S(1)} %get-tuple-element.43, f32[2048,4096]{1,0:T(8,128)} %select_add_fusion, s32[]{:T(128)S(6)} %add.113, f32[512,512]{0,1:T(8,128)} %get-tuple-element.100), kind=kOutput, calls=%fused_computation.13 | convolution fusion | flops 806092800 | bytes 4325380 | tf_op jit(solution)/shard_map/triangular_solve | solution.py:63
  284.1 6.9 %fusion.6 = f32[2048,128]{1,0:T(8,128)S(1)} fusion(f32[2048,128]{0,1:T(8,128)S(1)} %get-tuple-element.39, f32[2048,128]{0,1:T(8,128)S(1)} %get-tuple-element.41, f32[2048,128]{0,1:T(8,128)S(1)} %get-tuple-element.43, f32[2048,4096]{1,0:T(8,128)} %select_add_fusion, s32[]{:T(128)S(6)} %add.114, f32[512,512]{0,1:T(8,128)} %get-tuple-element.100), kind=kOutput, calls=%fused_computation.12 | convolution fusion | flops 1209794560 | bytes 5439492 | tf_op jit(solution)/shard_map/triangular_solve | solution.py:63
  294.0 86.3 %all-reduce.6.cloned.1.call-done = bf16[2048,512]{0,1:T(8,128)(2,1)} async-done(((bf16[2048,512]{0,1:T(8,128)(2,1)}), bf16[2048,512]{0,1:T(8,128)(2,1)}) %all-reduce.6.cloned.1.call-update) | async-done | bytes 2097168 | tf_op jit(solution)/shard_map/psum | solution.py:14
  380.3 3.9 convolution_bitcast_fusion
  384.2 3.9 copy.20
  388.1 31.2 %reduce-scatter.2.cloned.1.call-done = f32[512,64]{0,1:T(8,128)} async-done(((f32[512,512]{0,1:T(8,128)}), f32[512,64]{0,1:T(8,128)}) %reduce-scatter.2.cloned.1.call-update) | async-done | bytes 131088 | tf_op jit(solution)/shard_map/reduce_scatter | solution.py:69
  (73 shorter events, 43.0 us)
Async XLA Ops:
  7.2 373.2 %copy-start = (bf16[512,2048]{1,0:T(8,128)(2,1)S(1)}, bf16[512,2048]{1,0:T(8,128)(2,1)}, u32[]{:S(2)}) copy-start(bf16[512,2048]{1,0:T(8,128)(2,1)} %param.6) | copy-start | bytes 6291460
  7.2 71.9 %all-gather.2.cloned.1.call-start = ((), (), s32[]{:S(2)}) async-start(), calls=%async_computation.1 | async-start | bytes 9437184 | tf_op jit(solution)/shard_map/all_gather | solution.py:27
  25.6 217.7 %all-reduce.4.cloned.1.call-start = ((), (), s32[]{:S(2)}) async-start(), calls=%async_computation.2 | async-start | bytes 8388608 | tf_op jit(solution)/shard_map/psum | solution.py:14
  84.6 295.7 %all-reduce.6.cloned.1.call-start = ((), (), s32[]{:S(2)}) async-start(), calls=%async_computation.3 | async-start | bytes 4194304 | tf_op jit(solution)/shard_map/psum | solution.py:14
  92.1 1.0 copy-start.1
  294.0 125.4 %reduce-scatter.2.cloned.1.call-start = ((), (), s32[]{:S(2)}) async-start(), calls=%async_computation.4 | async-start | bytes 1179648 | tf_op jit(solution)/shard_map/reduce_scatter | solution.py:69
Sparse Core Ops, SparseCore 0:
  25.8 53.2 all-gather.1
  84.7 155.1 all-reduce.3
  294.1 86.1 all-reduce.5
  384.3 35.0 reduce-scatter.1
where the time goes:
time: 430 us; the launch traced here: 426 us
  other arithmetic  137 us (32%)
  waiting for transfers between devices  129 us (30%)
  matrix products  63 us (15%)
  blocking collectives  52.4 us (12%)
  local copies, waits for them, and re-layouts  25.1 us (6%)
  between operations  18.2 us (4%)
    psum x2, waiting for transfers between devices, broadcast(): return lax.psum(kept, axis)  86.3 us
    another operation x14, other arithmetic, on_device(): factor = jnp.linalg.cholesky(diag_block)  80.9 us
    another operation x3, other arithmetic, on_device(): lax.linalg.triangular_solve(factor, panel_rows, left_side=False, lower=Tr...  41.8 us
    psum x1, blocking collectives, on_device(): lax.psum(jnp.sum(normed_wide * normed_wide), ('seq', 'tensor')) / tokens_all  39 us
    reduce_scatter x1, waiting for transfers between devices, on_device(): lax.psum_scatter(partial_value, 'seq', scatter_dimension=1, tiled=True)  31.2 us
    dot_general x1, matrix products, on_device(): lax.dot_general(row_part, columns, (((0,), (0,)), ((), ())), preferred_el...  28.2 us
    another operation x7, matrix products, on_device(): lax.linalg.triangular_solve(factor, panel_rows, left_side=False, lower=Tr...  20.5 us
    another operation x20, local copies, waits for them, and re-layouts  14.3 us
  transfers between devices with their start and end apart: 4, of which 3 were waited for; matrix products, arithmetic and copies ran while one was open for 37% of the time, Pallas kernels for 0%

commit v1 on v0

--- a/solution.py
+++ b/solution.py
@@ -7,11 +7,14 @@
 PANEL = 512
 epsilon = 1e-05
 damping = 0.1
+play_trees_by_axis = lambda local_values, axis_tag: jnp.sum(
+    lax.all_gather(local_values, axis_tag), axis=0
+)
 
 
 def broadcast(value, axis, source):
     kept = jnp.where(lax.axis_index(axis) == source, value, 0).astype(value.dtype)
-    return lax.psum(kept, axis)
+    return play_trees_by_axis(kept, axis)
 
 
 def on_device(tokens, norm_gain, projection_weight, panel_index):

time: 430 us -> 642 us (1.49)
  waiting for transfers between devices: 129 us -> 310 us
  other arithmetic: 137 us -> 156 us
  blocking collectives: 52.4 us -> 65 us
    all_gather x0 -> x2, waiting for transfers between devices: none -> 223 us  [lax.all_gather(local_values, axis_tag)]
    psum x2 -> x0, waiting for transfers between devices: 86.3 us -> none  [broadcast(): return lax.psum(kept, axis)]
    all_gather x1, waiting for transfers between devices: 11.8 us -> 52.5 us  [on_device(): columns = lax.all_gather(normed, 'seq', axis=0, tiled=True)]
    psum x1, blocking collectives: 39 us -> 51.6 us  [on_device(): lax.psum(jnp.sum(normed_wide * normed_wide), ('seq', 'tensor')) / tokens_all]
    reduce_sum x0 -> x1, other arithmetic: none -> 12.1 us  [jnp.sum(lax.all_gather(local_values, axis_tag), axis=0)]
    unnamed x1 -> x2, other arithmetic: 0.01 us -> 6.63 us
    another operation x3 -> x6, other arithmetic: 41.8 us -> 42 us  [on_device(): lax.linalg.triangular_solve(factor, panel_rows, left_side=False, lower=Tr...]
  transfers between devices with their start and end apart: 4 -> 4, of which waited for: 3 -> 4; matrix products, arithmetic and copies ran while one was open for 37% -> 24% of each run, Pallas kernels for 0% -> 0%
where the time goes in v1:
time: 642 us; the launch traced here: 638 us
  waiting for transfers between devices  310 us (48%)
  other arithmetic  156 us (24%)
  blocking collectives  65 us (10%)
  matrix products  62.9 us (10%)
  local copies, waits for them, and re-layouts  25 us (4%)
  between operations  18.2 us (3%)
    all_gather x2, waiting for transfers between devices, lax.all_gather(local_values, axis_tag)  223 us
    another operation x14, other arithmetic, on_device(): factor = jnp.linalg.cholesky(diag_block)  81.3 us
    all_gather x1, waiting for transfers between devices, on_device(): columns = lax.all_gather(normed, 'seq', axis=0, tiled=True)  52.5 us
    psum x1, blocking collectives, on_device(): lax.psum(jnp.sum(normed_wide * normed_wide), ('seq', 'tensor')) / tokens_all  51.6 us
    another operation x6, other arithmetic, on_device(): lax.linalg.triangular_solve(factor, panel_rows, left_side=False, lower=Tr...  42 us
    reduce_scatter x1, waiting for transfers between devices, on_device(): lax.psum_scatter(partial_value, 'seq', scatter_dimension=1, tiled=True)  34.3 us
    dot_general x1, matrix products, on_device(): lax.dot_general(row_part, columns, (((0,), (0,)), ((), ())), preferred_el...  27.9 us
    another operation x7, matrix products, on_device(): lax.linalg.triangular_solve(factor, panel_rows, left_side=False, lower=Tr...  20.5 us
  transfers between devices with their start and end apart: 4, of which 4 were waited for; matrix products, arithmetic and copies ran while one was open for 24% of the time, Pallas kernels for 0%

profile of v1, /device:TPU:0, one launch (start us, length us, event | category | flops | bytes accessed | tf_op | source)
XLA Modules:
  0.0 637.9 jit_solution(15803451828422392584)
XLA Ops:
  8.9 13.5 %psum.14 = f32[128]{0:T(128)S(1)} all-reduce(f32[128]{0:T(128)S(1)} %fusion.10), channel_id=1, replica_groups=mesh['seq'=8,'tensor'=4] {'tensor'}, use_global_device_ids=true, to_apply=%region_1.0 | all-reduce | flops 128 | bytes 1024 | tf_op jit(solution)/shard_map/psum | solution.py:22
  25.7 52.5 %all-gather.5.cloned.1.call-done = bf16[1024,4096]{1,0:T(8,128)(2,1)} async-done(((bf16[128,4096]{1,0:T(8,128)(2,1)}), bf16[1024,4096]{1,0:T(8,128)(2,1)}) %all-gather.5.cloned.1.call-update) | async-done | bytes 8388624 | tf_op jit(solution)/shard_map/all_gather | solution.py:30
  78.3 5.5 dynamic-slice_select_fusion
  83.8 51.6 %psum.15 = f32[]{:T(128)} all-reduce(f32[]{:T(128)} %get-tuple-element.30), channel_id=1, replica_groups=mesh['seq'=8,'tensor'=4] {'seq','tensor'}, use_global_device_ids=true, to_apply=%region_4.5 | all-reduce | flops 1 | bytes 8 | tf_op jit(solution)/shard_map/psum | solution.py:41
  138.0 3.7 convert_select_fusion
  145.7 11.7 %cholesky.103 = f32[128,128]{1,0:T(8,128)S(1)} custom-call(f32[128,128]{1,0:T(8,128)S(1)} %cholesky.263), custom_call_target="Cholesky" | custom-call | tf_op jit(solution)/shard_map/jit(cholesky)/cholesky | solution.py:65
  158.8 9.8 %custom-call.30 = f32[1,128,128]{1,2,0:T(8,128)S(1)} custom-call(f32[1,128,128]{2,1,0:T(8,128)S(1)} %get-tuple-element.39), custom_call_target="InvertDiagBlocksLowerTriangular" | custom-call | tf_op jit(solution)/shard_map/jit(cholesky)/cholesky | solution.py:65
  171.2 11.7 %cholesky.215 = f32[128,128]{1,0:T(8,128)S(1)} custom-call(f32[128,128]{1,0:T(8,128)S(1)} %cholesky.267), custom_call_target="Cholesky" | custom-call | tf_op jit(solution)/shard_map/jit(cholesky)/cholesky | solution.py:65
  184.3 10.6 %custom-call.31 = f32[1,128,128]{1,2,0:T(8,128)} custom-call(f32[1,128,128]{2,1,0:T(8,128)S(1)} %get-tuple-element.37), custom_call_target="InvertDiagBlocksLowerTriangular" | custom-call | tf_op jit(solution)/shard_map/jit(cholesky)/cholesky | solution.py:65
  199.4 11.7 %cholesky.236 = f32[128,128]{1,0:T(8,128)S(1)} custom-call(f32[128,128]{1,0:T(8,128)S(1)} %cholesky.272), custom_call_target="Cholesky" | custom-call | tf_op jit(solution)/shard_map/jit(cholesky)/cholesky | solution.py:65
  211.3 9.8 %custom-call.32 = f32[1,128,128]{1,2,0:T(8,128)S(1)} custom-call(f32[1,128,128]{2,1,0:T(8,128)S(1)} %get-tuple-element.35), custom_call_target="InvertDiagBlocksLowerTriangular" | custom-call | tf_op jit(solution)/shard_map/jit(cholesky)/cholesky | solution.py:65
  222.7 12.1 %cholesky.253 = f32[128,128]{1,0:T(8,128)S(1)} custom-call(f32[128,128]{1,0:T(8,128)S(1)} %convolution_subtract_fusion.4), custom_call_target="Cholesky" | custom-call | tf_op jit(solution)/shard_map/jit(cholesky)/cholesky | solution.py:65
  242.0 14.3 %while.1 = (s32[]{:T(128)}, f32[512,512]{0,1:T(8,128)}, s32[4,2]{0,1:T(2,128)S(1)}, f32[4,128,128]{2,1,0:T(8,128)}, s32[]{:T(128)}) while((s32[]{:T(128)}, f32[512,512]{0,1:T(8,128)}, s32[4,2]{0,1:T(2,128)S(1)}, f32[4,128,128]{2,1,0:T(8,128)}, s32[]{:T(128)}) %tuple.32), condition=%wide.while_cond, body=%wide.while_body.sunk | while | flops 2 | bytes 393329 | solution.py:66
  256.3 40.1 %custom-call.33 = f32[4,128,128]{1,2,0:T(8,128)S(1)} custom-call(f32[4,128,128]{2,1,0:T(8,128)} %get-tuple-element.10), custom_call_target="InvertDiagBlocksLowerTriangular" | custom-call | tf_op jit(solution)/shard_map/triangular_solve | solution.py:66
  296.4 75.3 %all-gather.9.cloned.1.call-done = bf16[4096,2048]{1,0:T(8,128)(2,1)} async-done(((bf16[1024,2048]{1,0:T(8,128)(2,1)}), bf16[4096,2048]{1,0:T(8,128)(2,1)}) %all-gather.9.cloned.1.call-update) | async-done | bytes 16777232 | tf_op jit(solution)/shard_map/all_gather | solution.py:11
  371.7 12.1 %reduce_sum.43 = bf16[1024,2048]{1,0:T(8,128)(2,1)} reduce(bf16[4,1024,2048]{2,1,0:T(8,128)(2,1)} %bitcast.66, bf16[]{:T(256)} %constant.204.clone.1), dimensions={0}, to_apply=%region_2.3 | reduce | flops 6291456 | bytes 20971522 | tf_op jit(solution)/shard_map/reduce_sum | solution.py:10
  383.8 27.9 %select_add_fusion = f32[2048,4096]{1,0:T(8,128)} fusion(bf16[1024,2048]{1,0:T(8,128)(2,1)} %reduce_sum.43, bf16[1024,4096]{1,0:T(8,128)(2,1)} %all-gather.5.cloned.1.call-done, f32[]{:T(128)S(6)} %div.54, s32[4096]{0:T(1024)S(1)} %iota_add_fusion, s32[2048]{0:T(1024)S(1)} %copy-done.2), kind=kOutput, calls=%fused_computation.2 | convolution fusion | flops 17213423616 | bytes 46161924 | tf_op jit(solution)/shard_map/dot_general | solution.py:35
  418.4 5.0 convolution_subtract_fusion
  424.5 6.9 %fusion.6 = f32[2048,128]{1,0:T(8,128)S(1)} fusion(f32[2048,128]{0,1:T(8,128)S(1)} %fusion.30, f32[2048,128]{0,1:T(8,128)S(1)} %fusion.31, f32[2048,128]{0,1:T(8,128)S(1)} %fusion.16, f32[2048,4096]{1,0:T(8,128)} %select_add_fusion, s32[]{:T(128)S(6)} %add.110, f32[512,512]{0,1:T(8,128)} %get-tuple-element.100), kind=kOutput, calls=%fused_computation.12 | convolution fusion | flops 1209794560 | bytes 5439492 | tf_op jit(solution)/shard_map/triangular_solve | solution.py:66
  434.4 3.9 copy.33
  438.4 147.9 %all-gather.7.cloned.1.call-done = bf16[4,2048,512]{2,1,0:T(8,128)(2,1)} async-done(((bf16[1,2048,512]{2,1,0:T(8,128)(2,1)}), bf16[4,2048,512]{2,1,0:T(8,128)(2,1)}) %all-gather.7.cloned.1.call-update) | async-done | bytes 8388624 | tf_op jit(solution)/shard_map/all_gather | solution.py:11
  586.3 6.6 %reduce_sum.45 = bf16[2048,512]{1,0:T(8,128)(2,1)} reduce(bf16[4,2048,512]{2,1,0:T(8,128)(2,1)} %all-gather.7.cloned.1.call-done, bf16[]{:T(256)} %constant.204.clone.1), dimensions={0}, to_apply=%region_13.14 | reduce | flops 3145728 | bytes 10485762
  592.9 3.9 convolution_bitcast_fusion
  596.8 34.3 %reduce-scatter.2.cloned.1.call-done = f32[512,64]{0,1:T(8,128)} async-done(((f32[512,512]{0,1:T(8,128)}), f32[512,64]{0,1:T(8,128)}) %reduce-scatter.2.cloned.1.call-update) | async-done | bytes 131088 | tf_op jit(solution)/shard_map/reduce_scatter | solution.py:72
  (80 shorter events, 51.4 us)
Async XLA Ops:
  7.2 585.8 %copy-start = (bf16[512,2048]{1,0:T(8,128)(2,1)S(1)}, bf16[512,2048]{1,0:T(8,128)(2,1)}, u32[]{:S(2)}) copy-start(bf16[512,2048]{1,0:T(8,128)(2,1)} %param.6) | copy-start | bytes 6291460
  7.2 71.1 %all-gather.5.cloned.1.call-start = ((), (), s32[]{:S(2)}) async-start(), calls=%async_computation.1 | async-start | bytes 9437184 | tf_op jit(solution)/shard_map/all_gather | solution.py:30
  25.6 346.1 %all-gather.9.cloned.1.call-start = ((), (), s32[]{:S(2)}) async-start(), calls=%async_computation.4 | async-start | bytes 20971520 | tf_op jit(solution)/shard_map/all_gather | solution.py:11
  83.8 502.5 %all-gather.7.cloned.1.call-start = ((), (), s32[]{:S(2)}) async-start(), calls=%async_computation.2 | async-start | bytes 10485760 | tf_op jit(solution)/shard_map/all_gather | solution.py:11
  144.7 1.0 copy-start.1
  371.7 12.1 %copy-start.2 = (s32[2048]{0:T(1024)S(1)}, s32[2048]{0:T(1024)}, u32[]{:S(2)}) copy-start(s32[2048]{0:T(1024)} %iota_add_fusion.1) | copy-start | bytes 24580
  438.3 192.8 %reduce-scatter.2.cloned.1.call-start = ((), (), s32[]{:S(2)}) async-start(), calls=%async_computation.3 | async-start | bytes 1179648 | tf_op jit(solution)/shard_map/reduce_scatter | solution.py:72
Sparse Core Ops, SparseCore 0:
  25.8 52.4 all-gather.4
  83.9 287.7 all-gather.8
  438.4 147.7 all-gather.6
  596.9 34.1 reduce-scatter.1
